TPU v7x, 32 devices: a whole 2x2x4 slice. The times are simulated.
32 devices in a mesh: row: 8 (over y, x, core), col: 4 (over z).
Axes of the slice: x: 2, y: 2, z: 4, core: 2. Of those that a mesh axis runs over, the one named last changes fastest.
Arguments:
- matrix: float32 [16384, 16384], P('row', 'col'), may hold values from -8 to 8, as said below
- vectors: float32 [16384, 8192], P('row', 'col'), may hold values from -6 to 6
Outputs:
- updated: float32 [16384, 16384], P('row', 'col')
- rotated: float32 [16384, 8192], P('row', 'col')
Inputs may be any that keep to these rules, and one draw needn't show every extreme that they name: matrix is symmetric up to rounding.
All inputs are finite; a program needn't handle non-finite values.
Results may differ from a plain program's by a relative error of at most 0.00011.
Values sent between devices are 32-bit elements; how exact they have to be, the bound alone decides.
A program may use at most 192 MiB of HBM per device.

v0:
```python
import jax
import jax.numpy as jnp
from jax import lax
from jax.sharding import PartitionSpec as P

B = 256


def broadcast(array, axis, root):
    mine = lax.axis_index(axis) == root
    return lax.psum(jnp.where(mine, array, jnp.zeros_like(array)), axis)


def matmul(left, right):
    return jnp.dot(left, right, preferred_element_type=jnp.float32, precision=lax.Precision.HIGHEST)


def inner_product(left, right):
    return lax.dot_general(
        left,
        right,
        (((0,), (0,)), ((), ())),
        preferred_element_type=jnp.float32,
        precision=lax.Precision.HIGHEST,
    )


def outer_product(left, right):
    return lax.dot_general(
        left,
        right,
        (((1,), (1,)), ((), ())),
        preferred_element_type=jnp.float32,
        precision=lax.Precision.HIGHEST,
    )


def body(matrix, vectors):
    rows_here = matrix.shape[0]
    columns_here = matrix.shape[1]
    row_index = lax.axis_index("row")
    column_index = lax.axis_index("col")
    row_panel = broadcast(matrix[:, :B], "col", 0)
    column_panel = broadcast(matrix[:B, :], "row", 0)
    global_rows = row_index * rows_here + jnp.arange(rows_here, dtype=jnp.int32)
    global_columns = column_index * columns_here + jnp.arange(columns_here, dtype=jnp.int32)
    row_panel = jnp.where(global_rows[:, None] >= B, row_panel, jnp.float32(0.0))
    column_panel = jnp.where(global_columns[None, :] >= B, column_panel, jnp.float32(0.0))
    gram = lax.psum(inner_product(row_panel, row_panel), "row")
    factor = jnp.linalg.cholesky(gram)
    basis_rows = lax.linalg.triangular_solve(
        factor, row_panel, left_side=False, lower=True, transpose_a=True
    )
    basis_columns = lax.linalg.triangular_solve(
        factor, column_panel.T, left_side=False, lower=True, transpose_a=True
    )
    product_rows = lax.psum(matmul(matrix, basis_columns), "col")
    product_columns = lax.psum(inner_product(matrix, basis_rows), "row")
    coupling = lax.psum(inner_product(basis_rows, product_rows), "row")
    wide_rows = 2.0 * product_rows - 2.0 * matmul(basis_rows, coupling)
    wide_columns = 2.0 * product_columns - 2.0 * matmul(basis_columns, coupling)
    updated = (
        matrix - outer_product(basis_rows, wide_columns) - outer_product(wide_rows, basis_columns)
    )
    mixing = lax.psum(inner_product(basis_rows, vectors), "row")
    rotated = vectors - 2.0 * matmul(basis_rows, mixing)
    return (updated, rotated)


def solution(mesh):
    placed = (P("row", "col"), P("row", "col"))
    return jax.shard_map(
        body,
        mesh=mesh,
        in_specs=placed,
        out_specs=(P("row", "col"), P("row", "col")),
        check_vma=False,
    )
```

profile of v0, /device:TPU:0, one launch (start us, length us, event | category | flops | bytes accessed | tf_op | source)
XLA Modules:
  0.0 605.2 jit_solution(10097662528827411280)
XLA Ops:
  7.2 0.0 all-reduce.8.cloned.1.call-start
  7.2 3.0 slice_select_fusion.1
  10.3 0.0 all-reduce.8.cloned.1.call-update
  10.3 0.0 all-reduce.14.cloned.1.call-start
  10.4 4.6 slice_select_fusion
  15.0 84.8 %all-reduce.8.cloned.1.call-done = f32[2048,256]{1,0:T(8,128)} async-done(((f32[2048,256]{1,0:T(8,128)}), f32[2048,256]{1,0:T(8,128)}) %all-reduce.8.cloned.1.call-update) | async-done | bytes 2097168 | tf_op jit(solution)/shard_map/psum | solution.py:11
  99.8 1.9 broadcast_select_fusion
  101.7 4.2 fusion.27
  105.9 0.0 all-reduce.14.cloned.1.call-update
  105.9 0.5 all-reduce.10.cloned.1.call-start
  106.5 82.4 %all-reduce.14.cloned.1.call-done = (f32[256,4096]{1,0:T(8,128)}, f32[256,256]{0,1:T(8,128)}) async-done(((f32[256,4096]{1,0:T(8,128)}, f32[256,256]{0,1:T(8,128)}), (f32[256,4096]{1,0:T(8,128)}, f32[256,256]{0,1:T(8,128)})) %all-reduce.14.cloned.1.call-update) | async-done | bytes 4456464 | tf_op jit(solution)/shard_map/psum | solution.py:11
  188.8 1.1 copy.5
  189.9 1.0 fusion.6
  190.9 11.7 %cholesky.50 = f32[128,128]{1,0:T(8,128)S(1)} custom-call(f32[128,128]{1,0:T(8,128)S(1)} %cholesky.118), custom_call_target="Cholesky" | custom-call | tf_op jit(solution)/shard_map/jit(cholesky)/cholesky | solution.py:50
  202.7 9.8 %custom-call.16 = f32[1,128,128]{1,2,0:T(8,128)S(1)} custom-call(f32[1,128,128]{2,1,0:T(8,128)S(1)} %get-tuple-element.28), custom_call_target="InvertDiagBlocksLowerTriangular" | custom-call | tf_op jit(solution)/shard_map/jit(cholesky)/cholesky | solution.py:50
  212.5 0.2 constant_dynamic-update-slice_fusion.1
  212.7 0.3 convolution_subtract_fusion.2
  213.0 11.7 %cholesky.105 = f32[128,128]{1,0:T(8,128)S(1)} custom-call(f32[128,128]{1,0:T(8,128)S(1)} %convolution_subtract_fusion.2), custom_call_target="Cholesky" | custom-call | tf_op jit(solution)/shard_map/jit(cholesky)/cholesky | solution.py:50
  224.7 0.6 compare_reduce_fusion
  226.7 0.1 triangular_solve.73
  226.8 4.0 while.1
  226.8 0.6 fusion.46
  227.4 1.4 bitcast_dynamic-update-slice_fusion.2
  228.8 0.6 fusion.46
  229.4 1.4 bitcast_dynamic-update-slice_fusion.2
  230.8 19.8 %custom-call.17 = f32[2,128,128]{1,2,0:T(8,128)S(1)} custom-call(f32[2,128,128]{2,1,0:T(8,128)S(1)} %get-tuple-element.9), custom_call_target="InvertDiagBlocksLowerTriangular" | custom-call | tf_op jit(solution)/shard_map/triangular_solve | solution.py:51
  250.6 1.1 fusion.4
  251.7 0.0 copy-start.4
  251.7 1.8 convolution_subtract_fusion.1
  253.6 2.1 fusion.14
  255.7 0.0 copy-done.4
  255.7 0.5 select_bitcast_fusion
  256.1 2.0 fusion.2
  258.1 2.1 convolution_subtract_fusion
  260.2 2.0 fusion.13
  262.2 0.0 copy-start.2
  262.2 1.3 copy-done.2
  263.5 34.5 %convolution_bitcast_fusion.1 = f32[2048,256]{0,1:T(8,128)} fusion(f32[2048,4096]{1,0:T(8,128)} %param.2, f32[4096,128]{0,1:T(8,128)S(1)} %fusion.13, f32[4096,128]{0,1:T(8,128)S(1)} %fusion.2), kind=kOutput, calls=%fused_computation.13 | convolution fusion | flops 25770852352 | bytes 39845888 | tf_op jit(solution)/shard_map/dot_general | solution.py:15
  298.0 0.0 all-reduce.10.cloned.1.call-update
  298.1 0.0 all-reduce.12.cloned.1.call-start
  298.1 0.0 copy-start
  298.1 18.2 %fusion.7 = f32[256,2048]{1,0:T(8,128)} fusion(f32[2048,2048]{1,0:T(8,128)} %param.3, f32[2048,128]{0,1:T(8,128)} %fusion.14, f32[2048,128]{0,1:T(8,128)S(1)} %fusion.4), kind=kOutput, calls=%fused_computation.27 | convolution fusion | flops 12885426176 | bytes 20971520 | tf_op jit(solution)/shard_map/dot_general | solution.py:19
  316.4 0.0 copy-done
  316.4 33.8 %convolution_bitcast_fusion = f32[4096,256]{0,1:T(8,128)} fusion(f32[2048,4096]{1,0:T(8,128)} %param.2, f32[2048,128]{0,1:T(8,128)S(1)} %copy-done, f32[2048,128]{0,1:T(8,128)S(1)} %fusion.4), kind=kOutput, calls=%fused_computation.6 | convolution fusion | flops 25770328064 | bytes 39845888 | tf_op jit(solution)/shard_map/dot_general | solution.py:19
  350.2 34.2 %all-reduce.10.cloned.1.call-done = f32[2048,256]{0,1:T(8,128)} async-done(((f32[2048,256]{0,1:T(8,128)}), f32[2048,256]{0,1:T(8,128)}) %all-reduce.10.cloned.1.call-update) | async-done | bytes 2097168 | tf_op jit(solution)/shard_map/psum | solution.py:57
  384.4 4.5 fusion.9
  388.9 0.0 all-reduce.12.cloned.1.call-update
  388.9 106.1 %all-reduce.12.cloned.1.call-done = (f32[256,256]{1,0:T(8,128)}, f32[4096,256]{0,1:T(8,128)}, f32[256,2048]{1,0:T(8,128)}) async-done(((f32[256,256]{1,0:T(8,128)}, f32[4096,256]{0,1:T(8,128)}, f32[256,2048]{1,0:T(8,128)}), (f32[256,256]{1,0:T(8,128)}, f32[4096,256]{0,1:T(8,128)}, f32[256,2048]{1,0:T(8,128)})) %all-reduce.12.cloned.1.call-update) | async-done | bytes 6553616 | tf_op jit(solution)/shard_map/psum | solution.py:59
  495.0 0.0 copy-start.1
  495.0 7.3 %fusion = f32[4096,256]{0,1:T(8,128)S(1)} fusion(f32[256,256]{1,0:T(8,128)} %get-tuple-element.18, f32[4096,256]{0,1:T(8,128)} %get-tuple-element.19, f32[4096,128]{0,1:T(8,128)} %copy-done.2, f32[4096,128]{0,1:T(8,128)S(1)} %fusion.2), kind=kOutput, calls=%fused_computation.5 | convolution fusion | flops 3225419776 | bytes 12845056 | tf_op jit(solution)/shard_map/dot_general | solution.py:15
  502.3 0.0 copy-done.1
  502.3 0.0 copy-start.5
  502.3 30.7 %fusion.8 = f32[2048,4096]{1,0:T(8,128)} fusion(f32[4096,256]{0,1:T(8,128)S(1)} %fusion, f32[2048,128]{0,1:T(8,128)S(1)} %copy-done.1, f32[2048,128]{0,1:T(8,128)S(1)} %fusion.4), kind=kOutput, calls=%fused_computation.28 | convolution fusion | flops 25770328064 | bytes 39845888 | tf_op jit(solution)/shard_map/dot_general | solution.py:29
  533.0 0.0 copy-done.5
  533.0 0.0 copy-start.3
  533.0 0.0 copy-start.6
  533.0 19.2 %multiply_subtract_fusion = f32[2048,2048]{1,0:T(8,128)} fusion(f32[2048,2048]{1,0:T(8,128)} %param.3, f32[256,2048]{1,0:T(8,128)S(1)} %copy-done.5, f32[2048,128]{0,1:T(8,128)S(1)} %copy-done.1, f32[2048,128]{0,1:T(8,128)S(1)} %fusion.4), kind=kOutput, calls=%fused_computation.3 | convolution fusion | flops 12893814784 | bytes 37748736 | tf_op jit(solution)/shard_map/dot_general | solution.py:15
  552.3 0.0 copy-done.3
  552.3 0.0 copy-done.6
  552.3 3.5 fusion.1
  555.8 42.6 %subtract_subtract_fusion = f32[2048,4096]{1,0:T(8,128)} fusion(f32[2048,4096]{1,0:T(8,128)} %param.2, f32[2048,4096]{1,0:T(8,128)} %fusion.8, f32[2048,256]{0,1:T(8,128)} %fusion.1, f32[4096,128]{0,1:T(8,128)} %copy-done.2, f32[4096,128]{0,1:T(8,128)S(1)} %fusion.2), kind=kOutput, calls=%fused_computation.2 | convolution fusion | flops 25787629568 | bytes 106954752 | tf_op jit(solution)/shard_map/dot_general | solution.py:29
  (11 shorter events, 0.2 us)
Async XLA Ops:
  7.2 92.6 %all-reduce.8.cloned.1.call-start = ((), (), s32[]{:S(2)}) async-start(), calls=%async_computation | async-start | bytes 4194304 | tf_op jit(solution)/shard_map/psum | solution.py:11
  10.3 178.5 %all-reduce.14.cloned.1.call-start = ((), (), s32[]{:S(2)}) async-start(), calls=%async_computation.3 | async-start | bytes 8912896 | tf_op jit(solution)/shard_map/psum | solution.py:11
  105.9 278.5 %all-reduce.10.cloned.1.call-start = ((), (), s32[]{:S(2)}) async-start(), calls=%async_computation.1 | async-start | bytes 4194304 | tf_op jit(solution)/shard_map/psum | solution.py:57
  251.7 3.9 copy-start.4
  262.2 1.3 copy-start.2
  298.1 196.9 %all-reduce.12.cloned.1.call-start = ((), (), s32[]{:S(2)}) async-start(), calls=%async_computation.2 | async-start | bytes 13107200 | tf_op jit(solution)/shard_map/psum | solution.py:59
  298.1 18.3 %copy-start = (f32[2048,128]{0,1:T(8,128)S(1)}, f32[2048,128]{0,1:T(8,128)}, u32[]{:S(2)}) copy-start(f32[2048,128]{0,1:T(8,128)} %fusion.14) | copy-start | bytes 3145732
  495.0 7.3 %copy-start.1 = (f32[2048,128]{0,1:T(8,128)S(1)}, f32[2048,128]{0,1:T(8,128)}, u32[]{:S(2)}) copy-start(f32[2048,128]{0,1:T(8,128)} %fusion.14) | copy-start | bytes 3145732
  502.3 30.7 %copy-start.5 = (f32[256,2048]{1,0:T(8,128)S(1)}, f32[256,2048]{1,0:T(8,128)}, u32[]{:S(2)}) copy-start(f32[256,2048]{1,0:T(8,128)} %get-tuple-element.20) | copy-start | bytes 6291460
  533.0 19.3 %copy-start.3 = (f32[2048,256]{0,1:T(8,128)S(1)}, f32[2048,256]{0,1:T(8,128)}, u32[]{:S(2)}) copy-start(f32[2048,256]{0,1:T(8,128)} %all-reduce.10.cloned.1.call-done) | copy-start | bytes 6291460
  533.0 19.3 %copy-start.6 = (f32[256,256]{1,0:T(8,128)S(1)}, f32[256,256]{1,0:T(8,128)}, u32[]{:S(2)}) copy-start(f32[256,256]{1,0:T(8,128)} %get-tuple-element.18) | copy-start | bytes 786436
Sparse Core Ops, SparseCore 0:
  10.9 88.8 all-reduce.7
  106.0 82.7 all-reduce.13
  298.2 86.1 all-reduce.9
  389.0 105.9 all-reduce.11
where the time goes:
time: 609 us; the launch traced here: 605 us
  waiting for transfers between devices  308 us (51%)
  matrix products  210 us (34%)
  other arithmetic  64.9 us (11%)
  between operations  15.5 us (3%)
  local copies, waits for them, and re-layouts  6.46 us (1%)
    psum x2, waiting for transfers between devices, broadcast(): return lax.psum(jnp.where(mine, array, jnp.zeros_like(array)), axis)  167 us
    psum x1, waiting for transfers between devices, body(): coupling = lax.psum(inner_product(basis_rows, product_rows), 'row')  106 us
    dot_general x2, matrix products, outer_product(): lax.dot_general(left, right, (((1,), (1,)), ((), ())), preferred_element_...  73.4 us
    dot_general x4, matrix products, matmul(): jnp.dot(left, right, preferred_element_type=jnp.float32, precision=lax.Pr...  64.5 us
    dot_general x4, matrix products, inner_product(): lax.dot_general(left, right, (((0,), (0,)), ((), ())), preferred_element_...  60.7 us
    psum x1, waiting for transfers between devices, body(): product_rows = lax.psum(matmul(matrix, basis_columns), 'col')  34.2 us
    another operation x6, other arithmetic, body(): factor = jnp.linalg.cholesky(gram)  34 us
    another operation x3, other arithmetic, body(): lax.linalg.triangular_solve(factor, row_panel, left_side=False, lower=Tru...  19.9 us
  transfers between devices with their start and end apart: 4, of which 4 were waited for; matrix products, arithmetic and copies ran while one was open for 9% of the time, Pallas kernels for 0%

commit v1 on v0

--- a/solution.py
+++ b/solution.py
@@ -8,7 +8,7 @@
 
 def broadcast(array, axis, root):
     mine = lax.axis_index(axis) == root
-    return lax.psum(jnp.where(mine, array, jnp.zeros_like(array)), axis)
+    return jnp.sum(lax.all_gather(jnp.where(mine, array, jnp.zeros_like(array)), axis), axis=0)
 
 
 def matmul(left, right):

time: 609 us -> 760 us (1.25)
  waiting for transfers between devices: 308 us -> 434 us
  other arithmetic: 64.9 us -> 86.5 us
    all_gather x0 -> x2, waiting for transfers between devices: none -> 248 us  [broadcast(): lax.all_gather(jnp.where(mine, array, jnp.zeros_like(array)), axis)]
    psum x2 -> x1, waiting for transfers between devices: 167 us -> 47.1 us  [body(): gram = lax.psum(inner_product(row_panel, row_panel), 'row')]
    reduce_sum x0 -> x2, other arithmetic: none -> 19.7 us  [broadcast(): jnp.sum(lax.all_gather(jnp.where(mine, array, jnp.zeros_like(array)), axi...]
  transfers between devices with their start and end apart: 4 -> 5, of which waited for: 4 -> 5; matrix products, arithmetic and copies ran while one was open for 9% -> 16% of each run, Pallas kernels for 0% -> 0%
where the time goes in v1:
time: 760 us; the launch traced here: 755 us
  waiting for transfers between devices  434 us (57%)
  matrix products  211 us (28%)
  other arithmetic  86.5 us (11%)
  between operations  15.5 us (2%)
    all_gather x2, waiting for transfers between devices, broadcast(): lax.all_gather(jnp.where(mine, array, jnp.zeros_like(array)), axis)  248 us
    psum x1, waiting for transfers between devices, body(): coupling = lax.psum(inner_product(basis_rows, product_rows), 'row')  106 us
    dot_general x2, matrix products, outer_product(): lax.dot_general(left, right, (((1,), (1,)), ((), ())), preferred_element_...  73.6 us
    dot_general x4, matrix products, matmul(): jnp.dot(left, right, preferred_element_type=jnp.float32, precision=lax.Pr...  64.3 us
    dot_general x4, matrix products, inner_product(): lax.dot_general(left, right, (((0,), (0,)), ((), ())), preferred_element_...  61.6 us
    psum x1, waiting for transfers between devices, body(): gram = lax.psum(inner_product(row_panel, row_panel), 'row')  47.1 us
    another operation x6, other arithmetic, body(): factor = jnp.linalg.cholesky(gram)  34 us
    psum x1, waiting for transfers between devices, body(): product_rows = lax.psum(matmul(matrix, basis_columns), 'col')  33.3 us
  transfers between devices with their start and end apart: 5, of which 5 were waited for; matrix products, arithmetic and copies ran while one was open for 16% of the time, Pallas kernels for 0%

profile of v1, /device:TPU:0, one launch (start us, length us, event | category | flops | bytes accessed | tf_op | source)
XLA Modules:
  0.0 754.9 jit_solution(15186846126392545861)
XLA Ops:
  7.2 0.0 all-gather.5.cloned.1.call-start
  7.2 3.0 slice_select_fusion.1
  10.3 0.0 all-gather.5.cloned.1.call-update
  10.3 0.0 all-reduce.6.cloned.1.call-start
  10.4 152.4 %all-gather.5.cloned.1.call-done = f32[8192,256]{1,0:T(8,128)} async-done(((f32[2048,256]{1,0:T(8,128)}), f32[8192,256]{1,0:T(8,128)}) %all-gather.5.cloned.1.call-update) | async-done | bytes 8388624 | tf_op jit(solution)/shard_map/all_gather | solution.py:11
  162.8 5.5 reduce_sum.18
  168.3 1.9 broadcast_select_fusion
  170.2 4.2 fusion.27
  174.4 0.0 all-reduce.6.cloned.1.call-update
  174.4 0.0 all-gather.7.cloned.1.call-start
  174.5 4.6 slice_select_fusion
  179.1 0.0 all-gather.7.cloned.1.call-update
  179.1 0.3 all-reduce.8.cloned.1.call-start
  179.5 47.1 %all-reduce.6.cloned.1.call-done = f32[256,256]{0,1:T(8,128)} async-done(((f32[256,256]{0,1:T(8,128)}), f32[256,256]{0,1:T(8,128)}) %all-reduce.6.cloned.1.call-update) | async-done | bytes 262160 | tf_op jit(solution)/shard_map/psum | solution.py:49
  226.7 1.1 copy.5
  227.7 1.0 fusion.6
  228.7 11.7 %cholesky.50 = f32[128,128]{1,0:T(8,128)S(1)} custom-call(f32[128,128]{1,0:T(8,128)S(1)} %cholesky.118), custom_call_target="Cholesky" | custom-call | tf_op jit(solution)/shard_map/jit(cholesky)/cholesky | solution.py:50
  240.5 9.8 %custom-call.16 = f32[1,128,128]{1,2,0:T(8,128)S(1)} custom-call(f32[1,128,128]{2,1,0:T(8,128)S(1)} %get-tuple-element.26), custom_call_target="InvertDiagBlocksLowerTriangular" | custom-call | tf_op jit(solution)/shard_map/jit(cholesky)/cholesky | solution.py:50
  250.3 0.2 constant_dynamic-update-slice_fusion.1
  250.5 0.3 convolution_subtract_fusion.2
  250.8 11.7 %cholesky.105 = f32[128,128]{1,0:T(8,128)S(1)} custom-call(f32[128,128]{1,0:T(8,128)S(1)} %convolution_subtract_fusion.2), custom_call_target="Cholesky" | custom-call | tf_op jit(solution)/shard_map/jit(cholesky)/cholesky | solution.py:50
  262.6 0.7 compare_reduce_fusion
  264.6 0.1 triangular_solve.73
  264.7 4.4 while.1
  265.2 0.6 fusion.46
  265.8 1.4 bitcast_dynamic-update-slice_fusion.2
  267.2 0.6 fusion.46
  267.7 1.4 bitcast_dynamic-update-slice_fusion.2
  269.1 19.7 %custom-call.17 = f32[2,128,128]{1,2,0:T(8,128)S(1)} custom-call(f32[2,128,128]{2,1,0:T(8,128)S(1)} %get-tuple-element.9), custom_call_target="InvertDiagBlocksLowerTriangular" | custom-call | tf_op jit(solution)/shard_map/triangular_solve | solution.py:51
  288.8 1.1 fusion.4
  289.9 1.8 convolution_subtract_fusion.1
  291.7 2.1 fusion.14
  293.8 95.5 %all-gather.7.cloned.1.call-done = f32[2048,4096]{1,0:T(8,128)} async-done(((f32[256,4096]{1,0:T(8,128)}), f32[2048,4096]{1,0:T(8,128)}) %all-gather.7.cloned.1.call-update) | async-done | bytes 33554448 | tf_op jit(solution)/shard_map/all_gather | solution.py:11
  389.2 14.2 %reduce_sum.19 = f32[256,4096]{1,0:T(8,128)} reduce(f32[8,256,4096]{2,1,0:T(8,128)} %bitcast.54, f32[]{:T(128)} %constant.100.clone.1), dimensions={0}, to_apply=%region_7.8 | reduce | flops 7340032 | bytes 37748740 | tf_op jit(solution)/shard_map/reduce_sum | solution.py:11
  403.4 2.5 select_bitcast_fusion
  405.9 2.0 fusion.2
  407.9 2.1 convolution_subtract_fusion
  410.0 2.0 fusion.13
  412.0 0.0 copy-start.2
  412.0 1.3 copy-done.2
  413.3 34.3 %convolution_bitcast_fusion.1 = f32[2048,256]{0,1:T(8,128)} fusion(f32[2048,4096]{1,0:T(8,128)} %param.2, f32[4096,128]{0,1:T(8,128)S(1)} %fusion.13, f32[4096,128]{0,1:T(8,128)S(1)} %fusion.2), kind=kOutput, calls=%fused_computation.13 | convolution fusion | flops 25770852352 | bytes 39845888 | tf_op jit(solution)/shard_map/dot_general | solution.py:15
  447.6 0.0 all-reduce.8.cloned.1.call-update
  447.6 0.0 all-reduce.10.cloned.1.call-start
  447.7 0.0 copy-start
  447.7 19.2 %fusion.7 = f32[256,2048]{1,0:T(8,128)} fusion(f32[2048,2048]{1,0:T(8,128)} %param.3, f32[2048,128]{0,1:T(8,128)} %fusion.14, f32[2048,128]{0,1:T(8,128)S(1)} %fusion.4), kind=kOutput, calls=%fused_computation.27 | convolution fusion | flops 12885426176 | bytes 20971520 | tf_op jit(solution)/shard_map/dot_general | solution.py:19
  466.9 0.0 copy-done
  466.9 33.7 %convolution_bitcast_fusion = f32[4096,256]{0,1:T(8,128)} fusion(f32[2048,4096]{1,0:T(8,128)} %param.2, f32[2048,128]{0,1:T(8,128)S(1)} %copy-done, f32[2048,128]{0,1:T(8,128)S(1)} %fusion.4), kind=kOutput, calls=%fused_computation.6 | convolution fusion | flops 25770328064 | bytes 39845888 | tf_op jit(solution)/shard_map/dot_general | solution.py:19
  500.7 33.3 %all-reduce.8.cloned.1.call-done = f32[2048,256]{0,1:T(8,128)} async-done(((f32[2048,256]{0,1:T(8,128)}), f32[2048,256]{0,1:T(8,128)}) %all-reduce.8.cloned.1.call-update) | async-done | bytes 2097168 | tf_op jit(solution)/shard_map/psum | solution.py:57
  533.9 4.5 fusion.9
  538.4 0.0 all-reduce.10.cloned.1.call-update
  538.4 106.1 %all-reduce.10.cloned.1.call-done = (f32[256,256]{1,0:T(8,128)}, f32[4096,256]{0,1:T(8,128)}, f32[256,2048]{1,0:T(8,128)}) async-done(((f32[256,256]{1,0:T(8,128)}, f32[4096,256]{0,1:T(8,128)}, f32[256,2048]{1,0:T(8,128)}), (f32[256,256]{1,0:T(8,128)}, f32[4096,256]{0,1:T(8,128)}, f32[256,2048]{1,0:T(8,128)})) %all-reduce.10.cloned.1.call-update) | async-done | bytes 6553616 | tf_op jit(solution)/shard_map/psum | solution.py:59
  644.5 0.0 copy-start.1
  644.5 7.3 fusion
  651.8 0.0 copy-done.1
  651.8 0.0 copy-start.4
  651.8 31.0 %fusion.8 = f32[2048,4096]{1,0:T(8,128)} fusion(f32[4096,256]{0,1:T(8,128)S(1)} %fusion, f32[2048,128]{0,1:T(8,128)S(1)} %copy-done.1, f32[2048,128]{0,1:T(8,128)S(1)} %fusion.4), kind=kOutput, calls=%fused_computation.28 | convolution fusion | flops 25770328064 | bytes 39845888 | tf_op jit(solution)/shard_map/dot_general | solution.py:29
  682.8 0.0 copy-done.4
  682.8 0.0 copy-start.3
  682.8 0.0 copy-start.5
  682.8 19.2 %multiply_subtract_fusion = f32[2048,2048]{1,0:T(8,128)} fusion(f32[2048,2048]{1,0:T(8,128)} %param.3, f32[256,2048]{1,0:T(8,128)S(1)} %copy-done.4, f32[2048,128]{0,1:T(8,128)S(1)} %copy-done.1, f32[2048,128]{0,1:T(8,128)S(1)} %fusion.4), kind=kOutput, calls=%fused_computation.3 | convolution fusion | flops 12893814784 | bytes 37748736 | tf_op jit(solution)/shard_map/dot_general | solution.py:15
  702.1 0.0 copy-done.3
  702.1 0.0 copy-done.5
  702.1 3.5 fusion.1
  705.6 42.6 %subtract_subtract_fusion = f32[2048,4096]{1,0:T(8,128)} fusion(f32[2048,4096]{1,0:T(8,128)} %param.2, f32[2048,4096]{1,0:T(8,128)} %fusion.8, f32[2048,256]{0,1:T(8,128)} %fusion.1, f32[4096,128]{0,1:T(8,128)} %copy-done.2, f32[4096,128]{0,1:T(8,128)S(1)} %fusion.2), kind=kOutput, calls=%fused_computation.2 | convolution fusion | flops 25787629568 | bytes 106954752 | tf_op jit(solution)/shard_map/dot_general | solution.py:29
  (11 shorter events, 0.2 us)
Async XLA Ops:
  7.2 155.6 %all-gather.5.cloned.1.call-start = ((), (), s32[]{:S(2)}) async-start(), calls=%async_computation.2 | async-start | bytes 10485760 | tf_op jit(solution)/shard_map/all_gather | solution.py:11
  10.3 216.4 %all-reduce.6.cloned.1.call-start = ((), (), s32[]{:S(2)}) async-start(), calls=%async_computation | async-start | bytes 524288 | tf_op jit(solution)/shard_map/psum | solution.py:49
  174.4 214.8 %all-gather.7.cloned.1.call-start = ((), (), s32[]{:S(2)}) async-start(), calls=%async_computation.3 | async-start | bytes 37748736 | tf_op jit(solution)/shard_map/all_gather | solution.py:11
  179.1 354.8 %all-reduce.8.cloned.1.call-start = ((), (), s32[]{:S(2)}) async-start(), calls=%async_computation.1 | async-start | bytes 4194304 | tf_op jit(solution)/shard_map/psum | solution.py:57
  412.0 1.3 copy-start.2
  447.6 196.9 %all-reduce.10.cloned.1.call-start = ((), (), s32[]{:S(2)}) async-start(), calls=%async_computation.4 | async-start | bytes 13107200 | tf_op jit(solution)/shard_map/psum | solution.py:59
  447.7 19.3 %copy-start = (f32[2048,128]{0,1:T(8,128)S(1)}, f32[2048,128]{0,1:T(8,128)}, u32[]{:S(2)}) copy-start(f32[2048,128]{0,1:T(8,128)} %fusion.14) | copy-start | bytes 3145732
  644.5 7.3 copy-start.1
  651.8 31.0 %copy-start.4 = (f32[256,2048]{1,0:T(8,128)S(1)}, f32[256,2048]{1,0:T(8,128)}, u32[]{:S(2)}) copy-start(f32[256,2048]{1,0:T(8,128)} %get-tuple-element.20) | copy-start | bytes 6291460
  682.8 19.2 %copy-start.3 = (f32[2048,256]{0,1:T(8,128)S(1)}, f32[2048,256]{0,1:T(8,128)}, u32[]{:S(2)}) copy-start(f32[2048,256]{0,1:T(8,128)} %all-reduce.8.cloned.1.call-done) | copy-start | bytes 6291460
  682.8 19.2 %copy-start.5 = (f32[256,256]{1,0:T(8,128)S(1)}, f32[256,256]{1,0:T(8,128)}, u32[]{:S(2)}) copy-start(f32[256,256]{1,0:T(8,128)} %get-tuple-element.18) | copy-start | bytes 786436
Sparse Core Ops, SparseCore 0:
  10.4 152.3 all-gather.4
  174.5 52.0 all-reduce.5
  229.1 160.0 all-gather.6
  447.8 86.1 all-reduce.7
  538.6 105.9 all-reduce.9
